TPU v7x, 32 devices: a whole 2x2x4 slice. The times are simulated.
32 devices in a mesh: groups: 2 (over x), sub: 16 (over z, y, core).
Axes of the slice: x: 2, y: 2, z: 4, core: 2. Of those that a mesh axis runs over, the one named last changes fastest.
Arguments:
- modes_start: float32 [48, 6, 8192], P(None, None, ('groups', 'sub')), parts along dimension 2, may hold values from -6 to 6
- stiffness: float32 [24, 24, 8192], P(None, None, ('groups', 'sub')), parts along dimension 2, as said below
- mass: float32 [24, 24, 8192], P(None, None, ('groups', 'sub')), parts along dimension 2, as said below
- connect: int32 [4, 8192], P(None, ('groups', 'sub')), parts along dimension 1, may hold values from 0 to 382, as said below
Outputs:
- modes: float32 [48, 6, 8192], P(None, None, ('groups', 'sub')), parts along dimension 2
- ritz: float32 [96], P('groups'), parts along dimension 0
There are 2 independent parts, one for each index of `groups`. A program takes and returns all parts, laid end to end along the dimension named above; each array names one. Nothing has to cross between parts.
Inputs may be any that keep to these rules, and one draw needn't show every extreme that they name: `connect`: for element l of a subdomain, the four nodes are l + 64, one above it by less than 32, one below it by at most 64, and one above it by 32 or more and less than 64. `stiffness`: each block is symmetric positive definite. `mass`: each block is symmetric positive definite.
All inputs are finite; a program needn't handle non-finite values.
Results may differ from a plain program's by a relative error of at most 0.0001.
Values sent between devices are 32-bit elements; how exact they have to be, the bound alone decides.
No kernel may reach another device: no remote copies, remote signals or barrier semaphores. Data moves between devices by JAX's collectives and lax.ppermute only.
A program may use at most 64 MiB of HBM per device.

v0:
```python
import jax
import jax.numpy as jnp
from jax import lax
from jax.sharding import PartitionSpec as P

MODES = 48
HALO = 64
ITERS = 2
SMALL_STEPS = 2
highest = lax.Precision.HIGHEST


def with_halo(block, sides, width):
    for axis, dim in sides:
        count = lax.axis_size(axis)
        forward = [(i, i + 1) for i in range(count - 1)]
        backward = [(target, source) for source, target in forward]
        low = lax.ppermute(
            lax.slice_in_dim(block, block.shape[dim] - width, None, axis=dim), axis, forward
        )
        high = lax.ppermute(lax.slice_in_dim(block, 0, width, axis=dim), axis, backward)
        block = jnp.concatenate([low, block, high], axis=dim)
    return block


def shifted(value, axis, steps):
    count = lax.axis_size(axis)
    initial, last = (max(0, -steps), min(count, count - steps))
    return lax.ppermute(value, axis, [(source, source + steps) for source in range(initial, last)])


def inner(left, right):
    return jnp.einsum("acn,bcn->ab", left, right, precision=highest)


def combine(coeff, block):
    return jnp.einsum("ab,bcn->acn", coeff, block, precision=highest)


def symmetric(matrix):
    return 0.5 * (matrix + matrix.T)


def lower_solve(factor, rhs, transpose):
    return lax.linalg.triangular_solve(
        factor, rhs, left_side=True, lower=True, transpose_a=transpose
    )


def small_step(stiff_gram, mass_gram):
    scaling = 1.0 / jnp.sqrt(jnp.diagonal(mass_gram))
    outer = scaling[:, None] * scaling[None, :]
    stiff_scaled = symmetric(stiff_gram * outer)
    mass_scaled = symmetric(mass_gram * outer)
    factor = jnp.linalg.cholesky(stiff_scaled)
    coeff = jnp.eye(stiff_gram.shape[0], MODES, dtype=stiff_gram.dtype)
    for sweep in range(SMALL_STEPS):
        pushed = jnp.dot(mass_scaled, coeff, precision=highest)
        solved = lower_solve(factor, lower_solve(factor, pushed, False), True)
        normal_gram = symmetric(
            jnp.dot(solved.T, jnp.dot(mass_scaled, solved, precision=highest), precision=highest)
        )
        small_factor = jnp.linalg.cholesky(normal_gram)
        coeff = lower_solve(small_factor, solved.T, False).T
    return coeff * scaling[:, None]


def apply_pair(block, stiffness, mass, connect):
    rows = block.shape[0]
    count = block.shape[2]
    extended = with_halo(block, (("sub", 2),), HALO)
    width = count + 2 * HALO
    span = 128
    blocks = count // span
    window = span + 2 * HALO
    positions = jnp.arange(window, dtype=jnp.int32)
    stiff_blocks = stiffness.reshape(24, 24, blocks, span).transpose(2, 0, 1, 3)
    mass_blocks = mass.reshape(24, 24, blocks, span).transpose(2, 0, 1, 3)
    link_blocks = connect.reshape(4, blocks, span).transpose(1, 0, 2)

    def one_block(total, inputs):
        index, stiff_here, mass_here, link_here = inputs
        start = index * span
        local_window = lax.dynamic_slice_in_dim(extended, start, window, 2)
        selector = (link_here[:, :, None] - start == positions[None, None, :]).astype(block.dtype)
        picked = jnp.einsum("rcw,aew->rcae", local_window, selector, precision=highest).reshape(
            rows, 24, span
        )
        stiff_part = jnp.einsum("ije,rje->rie", stiff_here, picked, precision=highest)
        mass_part = jnp.einsum("ije,rje->rie", mass_here, picked, precision=highest)
        parts = jnp.stack([stiff_part, mass_part]).reshape(2, rows, 6, 4, span)
        placed = jnp.einsum("xrcae,aew->xrcw", parts, selector, precision=highest)
        old = lax.dynamic_slice_in_dim(total, start, window, 3)
        return (lax.dynamic_update_slice_in_dim(total, old + placed, start, 3), None)

    initial = jnp.zeros((2, rows, 6, width), block.dtype)
    summed, unused = lax.scan(
        one_block,
        initial,
        (jnp.arange(blocks, dtype=jnp.int32), stiff_blocks, mass_blocks, link_blocks),
    )
    from_below = shifted(summed[:, :, :, count + HALO :], "sub", 1)
    from_above = shifted(summed[:, :, :, :HALO], "sub", -1)
    inside = summed[:, :, :, HALO : count + HALO]
    inside = inside.at[:, :, :, :HALO].add(from_below)
    inside = inside.at[:, :, :, count - HALO :].add(from_above)
    return (inside[0], inside[1])


def body(modes_start, stiffness, mass, connect):
    stiff_start, mass_start = apply_pair(modes_start, stiffness, mass, connect)
    stiff_proj, mass_proj = lax.psum(
        (inner(modes_start, stiff_start), inner(modes_start, mass_start)), "sub"
    )
    factor = jnp.linalg.cholesky(symmetric(mass_proj))
    inverse = lower_solve(factor, jnp.eye(MODES, dtype=mass_proj.dtype), False)
    current = combine(inverse, modes_start)
    stiff_cur = combine(inverse, stiff_start)
    mass_cur = combine(inverse, mass_start)
    rayleigh = symmetric(
        jnp.dot(inverse, jnp.dot(stiff_proj, inverse.T, precision=highest), precision=highest)
    )
    direction = current
    stiff_dir = current
    mass_dir = current
    carried = rayleigh
    for sweep in range(ITERS):
        if sweep > 0:
            rayleigh = symmetric(lax.psum(inner(current, stiff_cur), "sub"))
        residual = stiff_cur - combine(rayleigh, mass_cur)
        stiff_res, mass_res = apply_pair(residual, stiffness, mass, connect)
        if sweep == 0:
            basis = jnp.concatenate([current, residual])
            stiff_basis = jnp.concatenate([stiff_cur, stiff_res])
            mass_basis = jnp.concatenate([mass_cur, mass_res])
        else:
            basis = jnp.concatenate([current, residual, direction])
            stiff_basis = jnp.concatenate([stiff_cur, stiff_res, stiff_dir])
            mass_basis = jnp.concatenate([mass_cur, mass_res, mass_dir])
        stiff_gram, mass_gram = lax.psum(
            (inner(basis, stiff_basis), inner(basis, mass_basis)), "sub"
        )
        coeff = small_step(stiff_gram, mass_gram)
        carried = symmetric(
            jnp.dot(coeff.T, jnp.dot(stiff_gram, coeff, precision=highest), precision=highest)
        )
        current = combine(coeff.T, basis)
        direction = combine(coeff[MODES:].T, basis[MODES:])
        if sweep + 1 < ITERS:
            stiff_cur = combine(coeff.T, stiff_basis)
            mass_cur = combine(coeff.T, mass_basis)
            stiff_dir = combine(coeff[MODES:].T, stiff_basis[MODES:])
            mass_dir = combine(coeff[MODES:].T, mass_basis[MODES:])
    return (current, jnp.diagonal(carried))


def solution(mesh):
    in_specs = (
        P(None, None, ("groups", "sub")),
        P(None, None, ("groups", "sub")),
        P(None, None, ("groups", "sub")),
        P(None, ("groups", "sub")),
    )
    out_specs = (P(None, None, ("groups", "sub")), P("groups"))
    return jax.shard_map(body, mesh=mesh, in_specs=in_specs, out_specs=out_specs, check_vma=False)
```

profile of v0, /device:TPU:0, one launch (start us, length us, event | category | flops | bytes accessed | tf_op | source)
XLA Modules:
  0.0 624.3 jit_solution(5031614352455597482)
XLA Ops:
  8.3 2.4 collective-permute-start
  12.2 3.1 copy.66
  19.5 33.1 %while.45 = (s32[]{:T(128)}, f32[2,48,6,384]{3,1,2,0:T(8,128)}, s32[2]{0:T(128)S(1)}, f32[48,6,384]{2,0,1:T(8,128)}, s32[2,4,128]{2,1,0:T(4,128)S(1)}, /*index=5...) while((s32[]{:T(128)}, f32[2,48,6,384]{3,1,2,0:T(8,128)}, ...), condition=%wide.region_1.2_spmd.clone, body=%wide.region_0.1_spmd.clone.sunk | while | flops 1444594176 | bytes 14656723 | solution.py:97
  22.8 4.0 fusion.320
  28.2 4.0 fusion.319
  33.3 2.7 fusion.321
  39.3 4.0 fusion.320
  44.8 4.0 fusion.319
  49.9 2.7 fusion.321
  53.9 5.2 collective-permute-start.2
  61.3 2.7 collective-permute-done.3
  64.1 2.3 scatter-add.21
  67.2 63.9 %all-reduce.6 = (f32[48,48]{1,0:T(8,128)S(1)}, f32[48,48]{0,1:T(8,128)S(1)}) all-reduce(f32[48,48]{1,0:T(8,128)S(1)} %convolution_bitcast_fusion.9, f32[48,48]{0,1:T(8,128)S(1)} %convolution_bitcast_fusion.8), channel_id=1, replica_groups=mesh['groups'=2,'sub'=16] {'sub'}, use_global_device_ids=true, to_apply=%region_2.3 | all-reduce | flops 4608 | bytes 36864 | tf_op jit(solution)/shard_map/psum | solution.py:112
  131.3 4.4 cholesky.251
  137.0 3.7 custom-call.37
  148.5 31.3 %while.46 = (s32[]{:T(128)}, f32[2,48,6,384]{3,1,2,0:T(8,128)}, s32[2]{0:T(128)S(1)}, f32[48,6,384]{2,0,1:T(8,128)S(1)}, s32[2,4,128]{2,1,0:T(4,128)S(1)}, /*ind...) while((s32[]{:T(128)}, f32[2,48,6,384]{3,1,2,0:T(8,128)}, ...), condition=%wide.region_7.9_spmd.clone, body=%wide.region_6.8_spmd.clone.sunk | while | flops 1444594176 | bytes 18195724 | solution.py:97
  151.0 4.0 fusion.332
  156.4 4.0 fusion.331
  161.5 2.7 fusion.333
  166.6 4.0 fusion.332
  172.0 4.0 fusion.331
  177.2 2.7 fusion.333
  181.1 2.9 collective-permute-start.6
  194.2 91.6 %all-reduce.11.cloned.1.call-done = (f32[96,96]{0,1:T(8,128)}, f32[96,96]{0,1:T(8,128)}) async-done(((f32[96,96]{0,1:T(8,128)}, f32[96,96]{0,1:T(8,128)}), (f32[96,96]{0,1:T(8,128)}, f32[96,96]{0,1:T(8,128)})) %all-reduce.11.cloned.1.call-update) | async-done | bytes 73744 | tf_op jit(solution)/shard_map/psum | solution.py:140
  289.3 8.8 %cholesky.95 = f32[96,96]{1,0:T(8,128)S(1)} custom-call(f32[96,96]{1,0:T(8,128)S(1)} %broadcast_multiply_fusion.1), custom_call_target="Cholesky" | custom-call | tf_op jit(solution)/shard_map/jit(cholesky)/cholesky | solution.py:55
  299.4 7.4 %custom-call.55 = f32[1,96,96]{1,2,0:T(8,128)S(1)} custom-call(f32[1,96,96]{2,1,0:T(8,128)S(1)} %fusion.104), custom_call_target="InvertDiagBlocksLowerTriangular" | custom-call | tf_op jit(solution)/shard_map/triangular_solve/custom-call.7 | solution.py:45
  308.1 4.4 cholesky.262
  313.8 3.7 custom-call.53
  319.0 4.4 cholesky.273
  324.7 3.7 custom-call.56
  331.5 58.5 %psum.53 = f32[48,48]{1,0:T(8,128)S(1)} all-reduce(f32[48,48]{1,0:T(8,128)S(1)} %convolution_bitcast_fusion.7), channel_id=1, replica_groups=mesh['groups'=2,'sub'=16] {'sub'}, use_global_device_ids=true, to_apply=%region_12.17 | all-reduce | flops 2304 | bytes 18432 | tf_op jit(solution)/shard_map/psum | solution.py:129
  397.2 33.2 %while.47 = (s32[]{:T(128)}, f32[2,48,6,384]{3,1,2,0:T(8,128)}, s32[2]{0:T(128)S(1)}, f32[48,6,384]{2,0,1:T(8,128)}, s32[2,4,128]{2,1,0:T(4,128)S(1)}, /*index=5...) while((s32[]{:T(128)}, f32[2,48,6,384]{3,1,2,0:T(8,128)}, ...), condition=%wide.region_14.19_spmd.clone, body=%wide.region_13.18_spmd.clone.sunk | while | flops 1444594176 | bytes 14656723 | solution.py:97
  400.6 4.0 fusion.344
  406.0 4.0 fusion.343
  411.2 2.7 fusion.345
  417.2 4.0 fusion.344
  422.7 4.0 fusion.343
  427.8 2.7 fusion.345
  431.7 2.9 collective-permute-start.10
  445.4 93.9 %all-reduce.13.cloned.1.call-done = (f32[144,144]{0,1:T(8,128)}, f32[144,144]{0,1:T(8,128)}) async-done(((f32[144,144]{0,1:T(8,128)}, f32[144,144]{0,1:T(8,128)}), (f32[144,144]{0,1:T(8,128)}, f32[144,144]{0,1:T(8,128)})) %all-reduce.13.cloned.1.call-update) | async-done | bytes 165904 | tf_op jit(solution)/shard_map/psum | solution.py:140
  539.3 3.2 gather_fusion.1
  544.4 11.7 %cholesky.155 = f32[128,128]{1,0:T(8,128)S(1)} custom-call(f32[128,128]{1,0:T(8,128)S(1)} %cholesky.304), custom_call_target="Cholesky" | custom-call | tf_op jit(solution)/shard_map/jit(cholesky)/cholesky | solution.py:55
  556.2 9.8 %custom-call.38 = f32[1,128,128]{1,2,0:T(8,128)S(1)} custom-call(f32[1,128,128]{2,1,0:T(8,128)S(1)} %get-tuple-element.375), custom_call_target="InvertDiagBlocksLowerTriangular" | custom-call | tf_op jit(solution)/shard_map/jit(cholesky)/cholesky | solution.py:55
  570.6 19.8 %custom-call.61 = f32[2,128,128]{1,2,0:T(8,128)S(1)} custom-call(f32[2,128,128]{2,1,0:T(8,128)S(1)} %pad_maximum_fusion.17), custom_call_target="InvertDiagBlocksLowerTriangular" | custom-call | tf_op jit(solution)/shard_map/triangular_solve/custom-call.10 | solution.py:45
  592.3 4.4 cholesky.284
  598.0 3.7 custom-call.59
  604.1 4.4 cholesky.295
  609.8 3.7 custom-call.62
  (295 shorter events, 108.1 us)
Async XLA Ops:
  7.2 278.7 %all-reduce.11.cloned.1.call-start = ((), (), s32[]{:S(2)}) async-start(), calls=%async_computation | async-start | bytes 196608 | tf_op jit(solution)/shard_map/psum | solution.py:140
  8.3 9.2 %collective-permute-start = (f32[48,6,64]{2,0,1:T(8,128)S(1)}, f32[48,6,64]{2,0,1:T(8,128)S(1)}, u32[]{:S(2)}, u32[]{:S(2)}) collective-permute-start(f32[48,6,64]{2,0,1:T(8,128)S(1)} %get-tuple-element.372), channel_id=1, source_target_pairs={{0,1},{1,2},{2,3},{3,4},{4,5},{5,6},{6,7},{7,8},{8,9},{9,10},{10,1... | collective-permute-start | bytes 221192 | tf_op jit(solution)/shard_map/ppermute | solution.py:18
  10.7 4.5 copy-start.23
  10.7 6.7 %collective-permute-start.1 = (f32[48,6,64]{2,0,1:T(8,128)S(1)}, f32[48,6,64]{2,0,1:T(8,128)S(1)}, u32[]{:S(2)}, u32[]{:S(2)}) collective-permute-start(f32[48,6,64]{2,0,1:T(8,128)S(1)} %get-tuple-element.373), channel_id=1, source_target_pairs={{1,0},{2,1},{3,2},{4,3},{5,4},{6,5},{7,6},{8,7},{9,8},{10,9},{11,1... | collective-permute-start | bytes 221192 | tf_op jit(solution)/shard_map/ppermute | solution.py:21
  15.2 2.2 copy-start.8
  17.5 2.0 copy-start.26
  32.3 1.1 copy-start
  48.8 1.1 copy-start
  52.6 6.5 %copy-start.3 = (f32[2,48,6,384]{3,1,2,0:T(8,128)S(1)}, f32[2,48,6,384]{3,1,2,0:T(8,128)}, u32[]{:S(2)}) copy-start(f32[2,48,6,384]{3,1,2,0:T(8,128)} %get-tuple-element.207) | copy-start | bytes 2654212
  53.9 6.7 %collective-permute-start.2 = (f32[2,48,6,64]{3,1,2,0:T(8,128)S(1)}, f32[2,48,6,64]{3,1,2,0:T(8,128)S(1)}, u32[]{:S(2)}, u32[]{:S(2)}) collective-permute-start(f32[2,48,6,64]{3,1,2,0:T(8,128)S(1)} %get-tuple-element.363), channel_id=1, source_target_pairs={{0,1},{1,2},{2,3},{3,4},{4,5},{5,6},{6,7},{7,8},{8,9},{9,10},{10,1... | collective-permute-start | bytes 442376 | tf_op jit(solution)/shard_map/ppermute | solution.py:29
  59.3 4.7 collective-permute-start.3
  141.3 6.2 copy-start.10
  141.7 6.8 %copy-start.12 = (f32[48,6,256]{2,0,1:T(8,128)}, f32[48,6,256]{2,0,1:T(8,128)S(1)}, u32[]{:S(2)}) copy-start(f32[48,6,256]{2,0,1:T(8,128)S(1)} %fusion.93) | copy-start | bytes 884740
  142.7 2.6 collective-permute-start.4
  144.0 3.3 collective-permute-start.5
  148.5 2.4 copy-start.6
  160.4 1.1 copy-start.1
  161.1 3.1 copy-start.7
  164.2 2.4 copy-start.6
  176.1 1.1 copy-start.1
  176.8 3.1 copy-start.7
  179.9 5.6 copy-start.4
  181.1 6.0 collective-permute-start.6
  185.6 3.5 collective-permute-start.7
  187.3 4.3 copy-start.13
  189.3 3.6 copy-start.11
  191.5 138.4 %copy-start.9 = (f32[2,48,6,256]{3,1,2,0:T(8,128)}, f32[2,48,6,256]{3,1,2,0:T(8,128)S(1)}, u32[]{:S(2)}) copy-start(f32[2,48,6,256]{3,1,2,0:T(8,128)S(1)} %scatter-add.25) | copy-start | bytes 1769476
  194.1 345.2 %all-reduce.13.cloned.1.call-start = ((), (), s32[]{:S(2)}) async-start(), calls=%async_computation.1 | async-start | bytes 589824 | tf_op jit(solution)/shard_map/psum | solution.py:140
  329.1 61.0 %copy-start.18 = (f32[48,6,256]{2,0,1:T(8,128)}, f32[48,6,256]{2,0,1:T(8,128)S(1)}, u32[]{:S(2)}) copy-start(f32[48,6,256]{2,0,1:T(8,128)S(1)} %fusion.90) | copy-start | bytes 884740
  329.5 61.0 %copy-start.16 = (f32[48,6,256]{2,0,1:T(8,128)}, f32[48,6,256]{2,0,1:T(8,128)S(1)}, u32[]{:S(2)}) copy-start(f32[48,6,256]{2,0,1:T(8,128)S(1)} %fusion.89) | copy-start | bytes 884740
  330.0 64.7 %copy-start.20 = (f32[48,6,256]{2,0,1:T(8,128)}, f32[48,6,256]{2,0,1:T(8,128)S(1)}, u32[]{:S(2)}) copy-start(f32[48,6,256]{2,0,1:T(8,128)S(1)} %fusion.88) | copy-start | bytes 884740
  390.5 4.7 copy-start.14
  390.7 4.0 collective-permute-start.8
  392.0 3.3 collective-permute-start.9
  410.1 1.1 copy-start.2
  426.7 1.1 copy-start.2
  430.5 5.6 copy-start.5
  431.7 6.3 %collective-permute-start.10 = (f32[2,48,6,64]{3,1,2,0:T(8,128)S(1)}, f32[2,48,6,64]{3,1,2,0:T(8,128)S(1)}, u32[]{:S(2)}, u32[]{:S(2)}) collective-permute-start(f32[2,48,6,64]{3,1,2,0:T(8,128)S(1)} %get-tuple-element.359), channel_id=1, source_target_pairs={{0,1},{1,2},{2,3},{3,4},{4,5},{5,6},{6,7},{7,8},{8,9},{9,10},{10,1... | collective-permute-start | bytes 442376 | tf_op jit(solution)/shard_map/ppermute | solution.py:29
  436.3 3.5 collective-permute-start.11
  438.2 4.1 copy-start.15
  438.2 4.1 copy-start.19
  438.2 4.1 copy-start.21
  438.2 4.1 copy-start.22
  438.2 4.1 copy-start.25
  442.2 1.6 copy-start.17
  570.5 43.2 %copy-start.24 = (f32[144,144]{0,1:T(8,128)S(1)}, f32[144,144]{0,1:T(8,128)}, u32[]{:S(2)}) copy-start(f32[144,144]{0,1:T(8,128)} %get-tuple-element.356) | copy-start | bytes 248836
Sparse Core Ops, SparseCore 0:
  194.2 91.5 all-reduce.10
  445.5 93.7 all-reduce.12
where the time goes:
time: 634 us; the launch traced here: 624 us
  waiting for transfers between devices  193 us (30%)
  blocking collectives  122 us (19%)
  other arithmetic  114 us (18%)
  matrix products  96 us (15%)
  local copies, waits for them, and re-layouts  52.9 us (8%)
  starting transfers between devices  24.7 us (4%)
  between operations  16.8 us (3%)
    psum x2, waiting for transfers between devices, body(): lax.psum((inner(basis, stiff_basis), inner(basis, mass_basis)), 'sub')  186 us
    psum x1, blocking collectives, body(): lax.psum((inner(modes_start, stiff_start), inner(modes_start, mass_start)...  63.9 us
    psum x1, blocking collectives, body(): rayleigh = symmetric(lax.psum(inner(current, stiff_cur), 'sub'))  58.5 us
    another operation x18, other arithmetic, lower_solve(): lax.linalg.triangular_solve(factor, rhs, left_side=True, lower=True, tran...  49.6 us
    another operation x10, other arithmetic, small_step(): factor = jnp.linalg.cholesky(stiff_scaled)  33.8 us
    dot_general x6, matrix products, one_block(): jnp.einsum('ije,rje->rie', stiff_here, picked, precision=highest)  24.3 us
    dot_general x6, matrix products, one_block(): mass_part = jnp.einsum('ije,rje->rie', mass_here, picked, precision=highest)  24.3 us
    another operation x12, other arithmetic, small_step(): small_factor = jnp.linalg.cholesky(normal_gram)  20.2 us
  transfers between devices with their start and end apart: 14, of which 7 were waited for; matrix products, arithmetic and copies ran while one was open for 2% of the time, Pallas kernels for 0%

commit v1 on v0

--- a/solution.py
+++ b/solution.py
@@ -126,7 +126,8 @@
     carried = rayleigh
     for sweep in range(ITERS):
         if sweep > 0:
-            rayleigh = symmetric(lax.psum(inner(current, stiff_cur), "sub"))
+            press_the_zones = lambda arr_in: jnp.sum(lax.all_gather(arr_in, "sub"), 0)
+            rayleigh = symmetric(press_the_zones(inner(current, stiff_cur)))
         residual = stiff_cur - combine(rayleigh, mass_cur)
         stiff_res, mass_res = apply_pair(residual, stiffness, mass, connect)
         if sweep == 0:

time: 634 us -> 600 us (0.946)
  blocking collectives: 122 us -> 84.4 us
    psum x1 -> x0, blocking collectives: 58.5 us -> none  [body(): rayleigh = symmetric(lax.psum(inner(current, stiff_cur), 'sub'))]
    all_gather x0 -> x1, blocking collectives: none -> 20.5 us  [body(): press_the_zones = lambda arr_in: jnp.sum(lax.all_gather(arr_in, 'sub'), 0)]
where the time goes in v1:
time: 600 us; the launch traced here: 590 us
  waiting for transfers between devices  193 us (32%)
  other arithmetic  114 us (19%)
  matrix products  96 us (16%)
  blocking collectives  84.4 us (14%)
  local copies, waits for them, and re-layouts  52.9 us (9%)
  starting transfers between devices  27.9 us (5%)
  between operations  16.8 us (3%)
    psum x2, waiting for transfers between devices, body(): lax.psum((inner(basis, stiff_basis), inner(basis, mass_basis)), 'sub')  186 us
    psum x1, blocking collectives, body(): lax.psum((inner(modes_start, stiff_start), inner(modes_start, mass_start)...  63.9 us
    another operation x18, other arithmetic, lower_solve(): lax.linalg.triangular_solve(factor, rhs, left_side=True, lower=True, tran...  49.6 us
    another operation x10, other arithmetic, small_step(): factor = jnp.linalg.cholesky(stiff_scaled)  33.8 us
    dot_general x6, matrix products, one_block(): jnp.einsum('ije,rje->rie', stiff_here, picked, precision=highest)  24.3 us
    dot_general x6, matrix products, one_block(): mass_part = jnp.einsum('ije,rje->rie', mass_here, picked, precision=highest)  24.2 us
    all_gather x1, blocking collectives, body(): press_the_zones = lambda arr_in: jnp.sum(lax.all_gather(arr_in, 'sub'), 0)  20.5 us
    another operation x12, other arithmetic, small_step(): small_factor = jnp.linalg.cholesky(normal_gram)  20.2 us
  transfers between devices with their start and end apart: 14, of which 7 were waited for; matrix products, arithmetic and copies ran while one was open for 2% of the time, Pallas kernels for 0%

profile of v1, /device:TPU:0, one launch (start us, length us, event | category | flops | bytes accessed | tf_op | source)
XLA Modules:
  0.0 589.7 jit_solution(11412868253818242789)
XLA Ops:
  8.3 2.4 collective-permute-start
  12.2 3.1 copy.66
  19.5 33.1 %while.45 = (s32[]{:T(128)}, f32[2,48,6,384]{3,1,2,0:T(8,128)}, s32[2]{0:T(128)S(1)}, f32[48,6,384]{2,0,1:T(8,128)}, s32[2,4,128]{2,1,0:T(4,128)S(1)}, /*index=5...) while((s32[]{:T(128)}, f32[2,48,6,384]{3,1,2,0:T(8,128)}, ...), condition=%wide.region_1.2_spmd.clone, body=%wide.region_0.1_spmd.clone.sunk | while | flops 1444594176 | bytes 14656723 | solution.py:97
  22.8 4.0 fusion.320
  28.2 4.0 fusion.319
  33.3 2.7 fusion.321
  39.3 4.0 fusion.320
  44.8 4.0 fusion.319
  49.9 2.7 fusion.321
  53.9 5.2 collective-permute-start.2
  61.3 2.7 collective-permute-done.3
  67.2 63.9 %all-reduce.6 = (f32[48,48]{1,0:T(8,128)S(1)}, f32[48,48]{0,1:T(8,128)S(1)}) all-reduce(f32[48,48]{1,0:T(8,128)S(1)} %convolution_bitcast_fusion.9, f32[48,48]{0,1:T(8,128)S(1)} %convolution_bitcast_fusion.8), channel_id=1, replica_groups=mesh['groups'=2,'sub'=16] {'sub'}, use_global_device_ids=true, to_apply=%region_2.3 | all-reduce | flops 4608 | bytes 36864 | tf_op jit(solution)/shard_map/psum | solution.py:112
  131.3 4.4 cholesky.251
  137.0 3.7 custom-call.37
  148.5 31.3 %while.46 = (s32[]{:T(128)}, f32[2,48,6,384]{3,1,2,0:T(8,128)}, s32[2]{0:T(128)S(1)}, f32[48,6,384]{2,0,1:T(8,128)S(1)}, s32[2,4,128]{2,1,0:T(4,128)S(1)}, /*ind...) while((s32[]{:T(128)}, f32[2,48,6,384]{3,1,2,0:T(8,128)}, ...), condition=%wide.region_7.9_spmd.clone, body=%wide.region_6.8_spmd.clone.sunk | while | flops 1444594176 | bytes 18195724 | solution.py:97
  151.0 4.0 fusion.332
  156.4 4.0 fusion.331
  161.5 2.7 fusion.333
  166.6 4.0 fusion.332
  172.0 4.0 fusion.331
  177.2 2.7 fusion.333
  181.1 2.9 collective-permute-start.6
  194.2 91.6 %all-reduce.11.cloned.1.call-done = (f32[96,96]{0,1:T(8,128)}, f32[96,96]{0,1:T(8,128)}) async-done(((f32[96,96]{0,1:T(8,128)}, f32[96,96]{0,1:T(8,128)}), (f32[96,96]{0,1:T(8,128)}, f32[96,96]{0,1:T(8,128)})) %all-reduce.11.cloned.1.call-update) | async-done | bytes 73744 | tf_op jit(solution)/shard_map/psum | solution.py:141
  289.3 8.8 %cholesky.95 = f32[96,96]{1,0:T(8,128)S(1)} custom-call(f32[96,96]{1,0:T(8,128)S(1)} %broadcast_multiply_fusion.1), custom_call_target="Cholesky" | custom-call | tf_op jit(solution)/shard_map/jit(cholesky)/cholesky | solution.py:55
  299.4 7.4 %custom-call.55 = f32[1,96,96]{1,2,0:T(8,128)S(1)} custom-call(f32[1,96,96]{2,1,0:T(8,128)S(1)} %fusion.104), custom_call_target="InvertDiagBlocksLowerTriangular" | custom-call | tf_op jit(solution)/shard_map/triangular_solve/custom-call.7 | solution.py:45
  308.1 4.4 cholesky.262
  313.8 3.7 custom-call.53
  319.0 4.4 cholesky.273
  324.7 3.7 custom-call.56
  331.5 20.5 %all-gather = f32[768,48]{1,0:T(8,128)S(1)} all-gather(f32[48,48]{1,0:T(8,128)S(1)} %convolution_bitcast_fusion.7), channel_id=2, replica_groups=mesh['groups'=2,'sub'=16] {'sub'}, dimensions={0}, use_global_device_ids=true | all-gather | bytes 156672 | tf_op jit(solution)/shard_map/all_gather | solution.py:129
  352.7 2.3 collective-permute-start.8
  360.2 33.2 %while.47 = (s32[]{:T(128)}, f32[2,48,6,384]{3,1,2,0:T(8,128)}, s32[2]{0:T(128)S(1)}, f32[48,6,384]{2,0,1:T(8,128)}, s32[2,4,128]{2,1,0:T(4,128)S(1)}, /*index=5...) while((s32[]{:T(128)}, f32[2,48,6,384]{3,1,2,0:T(8,128)}, ...), condition=%wide.region_14.19_spmd.clone, body=%wide.region_13.18_spmd.clone.sunk | while | flops 1444594176 | bytes 14656723 | solution.py:97
  363.5 4.0 fusion.344
  369.0 4.0 fusion.343
  374.1 2.7 fusion.345
  380.2 4.0 fusion.344
  385.6 4.0 fusion.343
  390.8 2.7 fusion.345
  394.7 5.1 collective-permute-start.10
  410.6 94.1 %all-reduce.13.cloned.1.call-done = (f32[144,144]{0,1:T(8,128)}, f32[144,144]{0,1:T(8,128)}) async-done(((f32[144,144]{0,1:T(8,128)}, f32[144,144]{0,1:T(8,128)}), (f32[144,144]{0,1:T(8,128)}, f32[144,144]{0,1:T(8,128)})) %all-reduce.13.cloned.1.call-update) | async-done | bytes 165904 | tf_op jit(solution)/shard_map/psum | solution.py:141
  504.7 3.2 gather_fusion.1
  509.8 11.7 %cholesky.155 = f32[128,128]{1,0:T(8,128)S(1)} custom-call(f32[128,128]{1,0:T(8,128)S(1)} %cholesky.304), custom_call_target="Cholesky" | custom-call | tf_op jit(solution)/shard_map/jit(cholesky)/cholesky | solution.py:55
  521.6 9.8 %custom-call.38 = f32[1,128,128]{1,2,0:T(8,128)S(1)} custom-call(f32[1,128,128]{2,1,0:T(8,128)S(1)} %get-tuple-element.375), custom_call_target="InvertDiagBlocksLowerTriangular" | custom-call | tf_op jit(solution)/shard_map/jit(cholesky)/cholesky | solution.py:55
  535.9 19.8 %custom-call.61 = f32[2,128,128]{1,2,0:T(8,128)S(1)} custom-call(f32[2,128,128]{2,1,0:T(8,128)S(1)} %pad_maximum_fusion.17), custom_call_target="InvertDiagBlocksLowerTriangular" | custom-call | tf_op jit(solution)/shard_map/triangular_solve/custom-call.10 | solution.py:45
  557.6 4.4 cholesky.284
  563.4 3.7 custom-call.59
  569.4 4.4 cholesky.295
  575.2 3.7 custom-call.62
  (296 shorter events, 109.0 us)
Async XLA Ops:
  7.2 278.7 %all-reduce.11.cloned.1.call-start = ((), (), s32[]{:S(2)}) async-start(), calls=%async_computation | async-start | bytes 196608 | tf_op jit(solution)/shard_map/psum | solution.py:141
  8.3 9.2 %collective-permute-start = (f32[48,6,64]{2,0,1:T(8,128)S(1)}, f32[48,6,64]{2,0,1:T(8,128)S(1)}, u32[]{:S(2)}, u32[]{:S(2)}) collective-permute-start(f32[48,6,64]{2,0,1:T(8,128)S(1)} %get-tuple-element.372), channel_id=1, source_target_pairs={{0,1},{1,2},{2,3},{3,4},{4,5},{5,6},{6,7},{7,8},{8,9},{9,10},{10,1... | collective-permute-start | bytes 221192 | tf_op jit(solution)/shard_map/ppermute | solution.py:18
  10.7 4.5 copy-start.23
  10.7 6.7 %collective-permute-start.1 = (f32[48,6,64]{2,0,1:T(8,128)S(1)}, f32[48,6,64]{2,0,1:T(8,128)S(1)}, u32[]{:S(2)}, u32[]{:S(2)}) collective-permute-start(f32[48,6,64]{2,0,1:T(8,128)S(1)} %get-tuple-element.373), channel_id=1, source_target_pairs={{1,0},{2,1},{3,2},{4,3},{5,4},{6,5},{7,6},{8,7},{9,8},{10,9},{11,1... | collective-permute-start | bytes 221192 | tf_op jit(solution)/shard_map/ppermute | solution.py:21
  15.2 2.2 copy-start.8
  17.5 2.0 copy-start.26
  32.3 1.1 copy-start
  48.8 1.1 copy-start
  52.6 6.5 %copy-start.3 = (f32[2,48,6,384]{3,1,2,0:T(8,128)S(1)}, f32[2,48,6,384]{3,1,2,0:T(8,128)}, u32[]{:S(2)}) copy-start(f32[2,48,6,384]{3,1,2,0:T(8,128)} %get-tuple-element.207) | copy-start | bytes 2654212
  53.9 6.7 %collective-permute-start.2 = (f32[2,48,6,64]{3,1,2,0:T(8,128)S(1)}, f32[2,48,6,64]{3,1,2,0:T(8,128)S(1)}, u32[]{:S(2)}, u32[]{:S(2)}) collective-permute-start(f32[2,48,6,64]{3,1,2,0:T(8,128)S(1)} %get-tuple-element.363), channel_id=1, source_target_pairs={{0,1},{1,2},{2,3},{3,4},{4,5},{5,6},{6,7},{7,8},{8,9},{9,10},{10,1... | collective-permute-start | bytes 442376 | tf_op jit(solution)/shard_map/ppermute | solution.py:29
  59.3 4.7 collective-permute-start.3
  141.3 6.2 %copy-start.10 = (f32[48,6,256]{2,0,1:T(8,128)}, f32[48,6,256]{2,0,1:T(8,128)S(1)}, u32[]{:S(2)}) copy-start(f32[48,6,256]{2,0,1:T(8,128)S(1)} %fusion.92) | copy-start | bytes 884740
  141.7 6.8 %copy-start.12 = (f32[48,6,256]{2,0,1:T(8,128)}, f32[48,6,256]{2,0,1:T(8,128)S(1)}, u32[]{:S(2)}) copy-start(f32[48,6,256]{2,0,1:T(8,128)S(1)} %fusion.93) | copy-start | bytes 884740
  142.7 2.6 collective-permute-start.4
  144.0 3.3 collective-permute-start.5
  148.5 2.4 copy-start.6
  160.4 1.1 copy-start.1
  161.1 3.1 copy-start.7
  164.2 2.4 copy-start.6
  176.1 1.1 copy-start.1
  176.8 3.1 copy-start.7
  179.9 5.6 copy-start.4
  181.1 6.0 %collective-permute-start.6 = (f32[2,48,6,64]{3,1,2,0:T(8,128)S(1)}, f32[2,48,6,64]{3,1,2,0:T(8,128)S(1)}, u32[]{:S(2)}, u32[]{:S(2)}) collective-permute-start(f32[2,48,6,64]{3,1,2,0:T(8,128)S(1)} %get-tuple-element.361), channel_id=1, source_target_pairs={{0,1},{1,2},{2,3},{3,4},{4,5},{5,6},{6,7},{7,8},{8,9},{9,10},{10,1... | collective-permute-start | bytes 442376 | tf_op jit(solution)/shard_map/ppermute | solution.py:29
  185.6 3.5 collective-permute-start.7
  187.3 4.3 copy-start.13
  189.3 3.6 copy-start.11
  191.5 138.4 %copy-start.9 = (f32[2,48,6,256]{3,1,2,0:T(8,128)}, f32[2,48,6,256]{3,1,2,0:T(8,128)S(1)}, u32[]{:S(2)}) copy-start(f32[2,48,6,256]{3,1,2,0:T(8,128)S(1)} %scatter-add.25) | copy-start | bytes 1769476
  194.1 310.5 %all-reduce.13.cloned.1.call-start = ((), (), s32[]{:S(2)}) async-start(), calls=%async_computation.1 | async-start | bytes 589824 | tf_op jit(solution)/shard_map/psum | solution.py:141
  329.1 22.9 %copy-start.18 = (f32[48,6,256]{2,0,1:T(8,128)}, f32[48,6,256]{2,0,1:T(8,128)S(1)}, u32[]{:S(2)}) copy-start(f32[48,6,256]{2,0,1:T(8,128)S(1)} %fusion.90) | copy-start | bytes 884740
  329.5 23.0 %copy-start.16 = (f32[48,6,256]{2,0,1:T(8,128)}, f32[48,6,256]{2,0,1:T(8,128)S(1)}, u32[]{:S(2)}) copy-start(f32[48,6,256]{2,0,1:T(8,128)S(1)} %fusion.89) | copy-start | bytes 884740
  330.0 22.7 %copy-start.20 = (f32[48,6,256]{2,0,1:T(8,128)}, f32[48,6,256]{2,0,1:T(8,128)S(1)}, u32[]{:S(2)}) copy-start(f32[48,6,256]{2,0,1:T(8,128)S(1)} %fusion.88) | copy-start | bytes 884740
  352.6 5.7 copy-start.14
  352.7 4.9 collective-permute-start.8
  355.0 3.3 collective-permute-start.9
  373.1 1.1 copy-start.2
  389.7 1.1 copy-start.2
  393.5 7.8 %copy-start.5 = (f32[2,48,6,384]{3,1,2,0:T(8,128)S(1)}, f32[2,48,6,384]{3,1,2,0:T(8,128)}, u32[]{:S(2)}) copy-start(f32[2,48,6,384]{3,1,2,0:T(8,128)} %get-tuple-element.209) | copy-start | bytes 2654212
  394.7 8.5 %collective-permute-start.10 = (f32[2,48,6,64]{3,1,2,0:T(8,128)S(1)}, f32[2,48,6,64]{3,1,2,0:T(8,128)S(1)}, u32[]{:S(2)}, u32[]{:S(2)}) collective-permute-start(f32[2,48,6,64]{3,1,2,0:T(8,128)S(1)} %get-tuple-element.359), channel_id=1, source_target_pairs={{0,1},{1,2},{2,3},{3,4},{4,5},{5,6},{6,7},{7,8},{8,9},{9,10},{10,1... | collective-permute-start | bytes 442376 | tf_op jit(solution)/shard_map/ppermute | solution.py:29
  401.5 3.5 collective-permute-start.11
  403.4 4.1 copy-start.15
  403.4 4.1 copy-start.19
  403.4 4.1 copy-start.21
  403.4 4.1 copy-start.22
  403.4 4.1 copy-start.25
  407.4 1.6 copy-start.17
  535.9 43.2 %copy-start.24 = (f32[144,144]{0,1:T(8,128)S(1)}, f32[144,144]{0,1:T(8,128)}, u32[]{:S(2)}) copy-start(f32[144,144]{0,1:T(8,128)} %get-tuple-element.356) | copy-start | bytes 248836
Sparse Core Ops, SparseCore 0:
  194.2 91.5 all-reduce.10
  410.7 93.9 all-reduce.12
